TPU v7x, 32 devices: a whole 2x2x4 slice. The times are simulated.
32 devices in a mesh: groups: 2 (over y), seq: 4 (over z), inner: 2 (over x), batch: 2 (over core).
Axes of the slice: x: 2, y: 2, z: 4, core: 2. Of those that a mesh axis runs over, the one named last changes fastest.
Arguments:
- queries: bfloat16 [4, 2048, 256], P(('groups', 'batch'), ('seq', 'inner')), parts along dimension 0, may hold values from -6 to 6
- keys: bfloat16 [4, 2048, 256], P(('groups', 'batch'), ('seq', 'inner')), parts along dimension 0, may hold values from -6 to 6
- values: bfloat16 [4, 2048, 256], P(('groups', 'batch'), ('seq', 'inner')), parts along dimension 0, may hold values from -6 to 6
- rates: float32 [4, 2048], P(('groups', 'batch'), ('seq', 'inner')), parts along dimension 0, may hold values from 0.05 to 1
- video_start: int32 [4], P(('groups', 'batch')), parts along dimension 0, may hold values from 0 to 511
- span_len: int32 [4, 4], P(('groups', 'batch'), 'seq'), parts along dimension 0, may hold values from 256 to 512, as said below
- init_weights: float32 [3, 256, 256], replicated, may hold values from -0.375 to 0.375
Outputs:
- outputs: bfloat16 [4, 2048, 256], P(('groups', 'batch'), ('seq', 'inner')), parts along dimension 0
- final_weights: float32 [4, 3, 256, 256], P(('groups', 'batch'), None, 'seq'), parts along dimension 0
There are 2 independent parts, one for each index of `groups`. A program takes and returns all parts, laid end to end along the dimension named above; an argument that names none is the same for every part. Nothing has to cross between parts.
Inputs may be any that keep to these rules, and one draw needn't show every extreme that they name: Every video has at least one span with span_len equal to 512.
All inputs are finite; a program needn't handle non-finite values.
Results may differ from a plain program's by a relative error of at most 0.015.
Values may be sent and summed in bfloat16 or wider, within the bound.
A program may use at most 64 MiB of HBM per device.

v0:
```python
import jax
import jax.numpy as jnp
from jax import lax
from jax.sharding import PartitionSpec as P

NS_STEPS = 5
step_size = 0.1
norm_eps = 1e-07
column_eps = 1e-06


def shifted(value, axis, steps):
    count = lax.axis_size(axis)
    initial, last = (max(0, -steps), min(count, count - steps))
    return lax.ppermute(value, axis, [(source, source + steps) for source in range(initial, last)])


def broadcast(value, axis, root):
    mine = lax.axis_index(axis) == root
    return lax.psum(jnp.where(mine, value, jnp.zeros_like(value)), axis)


def swish_parts(pre_act):
    sigma = jax.nn.sigmoid(pre_act)
    return (pre_act * sigma, sigma * (1.0 + pre_act * (1.0 - sigma)))


def apply_net(rows, half_weights):
    gate_pre = jnp.dot(rows, half_weights[0], preferred_element_type=jnp.float32)
    up_pre = jnp.dot(rows, half_weights[1], preferred_element_type=jnp.float32)
    active_part, unused_slope = swish_parts(gate_pre)
    hidden = (active_part * up_pre).astype(jnp.bfloat16)
    contract = (((1,), (1,)), ((), ()))
    return lax.dot_general(
        hidden, half_weights[2], contract, preferred_element_type=jnp.float32
    ).astype(jnp.bfloat16)


def key_grads(key_rows, value_rows, weight, half_weights):
    gate_pre = jnp.dot(key_rows, half_weights[0], preferred_element_type=jnp.float32)
    up_pre = jnp.dot(key_rows, half_weights[1], preferred_element_type=jnp.float32)
    active_part, slope_term = swish_parts(gate_pre)
    hidden = (active_part * up_pre).astype(jnp.bfloat16)
    neg_values = (-(weight[:, None] * value_rows.astype(jnp.float32))).astype(jnp.bfloat16)
    back_grad = jnp.dot(neg_values, half_weights[2], preferred_element_type=jnp.float32)
    d_upper = (back_grad * active_part).astype(jnp.bfloat16)
    d_gate = (back_grad * up_pre * slope_term).astype(jnp.bfloat16)
    contract = (((0,), (0,)), ((), ()))
    grad_one = lax.dot_general(key_rows, d_gate, contract, preferred_element_type=jnp.float32)
    grad_three = lax.dot_general(key_rows, d_upper, contract, preferred_element_type=jnp.float32)
    grad_two = lax.dot_general(neg_values, hidden, contract, preferred_element_type=jnp.float32)
    return jnp.stack([grad_one, grad_three, grad_two])


def newton(grad):
    scale = jnp.sqrt(jnp.sum(grad * grad))
    iterate = grad / (scale + norm_eps)
    for unused in range(NS_STEPS):
        gram = jnp.dot(
            iterate, iterate.T, precision=lax.Precision.HIGHEST, preferred_element_type=jnp.float32
        )
        iterate = 1.5 * iterate - 0.5 * jnp.dot(
            gram, iterate, precision=lax.Precision.HIGHEST, preferred_element_type=jnp.float32
        )
    return iterate.astype(jnp.bfloat16)


def renorm(before, moved):
    old_norm = jnp.sqrt(jnp.sum(before * before, axis=1, keepdims=True) + column_eps)
    new_norm = jnp.sqrt(jnp.sum(moved * moved, axis=1, keepdims=True) + column_eps)
    return moved * (old_norm / new_norm)


def ortho_all(total):
    return jax.vmap(newton)(total)


def ortho_none(total):
    return jnp.zeros(total.shape, jnp.bfloat16)


def pad_slots(array, slot_total):
    filler = jnp.zeros((slot_total - array.shape[0],) + tuple(array.shape[1:]), array.dtype)
    return jnp.concatenate([array, filler], axis=0)


def per_device(queries, keys, values, rates, video_start, span_len, init_weights):
    video_count, tok_rows, head_width = queries.shape
    seq_count = lax.axis_size("seq")
    inner_count = lax.axis_size("inner")
    seq_place = lax.axis_index("seq")
    inner_place = lax.axis_index("inner")
    span_rows = tok_rows * inner_count
    within = jnp.arange(tok_rows, dtype=jnp.int32) + inner_place * tok_rows
    state_shape = init_weights.shape
    per_owner = (state_shape[0] + inner_count - 1) // inner_count
    slot_total = per_owner * inner_count

    def local_terms(video_slot, state):
        half_weights = state.astype(jnp.bfloat16)
        query_rows = lax.dynamic_index_in_dim(queries, video_slot, 0, keepdims=False)
        key_rows = lax.dynamic_index_in_dim(keys, video_slot, 0, keepdims=False)
        value_rows = lax.dynamic_index_in_dim(values, video_slot, 0, keepdims=False)
        rate_rows = lax.dynamic_index_in_dim(rates, video_slot, 0, keepdims=False)
        length = lax.dynamic_index_in_dim(span_len, video_slot, 0, keepdims=False)[0]
        begin = lax.dynamic_index_in_dim(video_start, video_slot, 0, keepdims=False)
        position = seq_place * span_rows + within
        valid = ((position >= begin) & (within < length)).astype(jnp.float32)
        weight = rate_rows * valid
        partial_value = (
            key_grads(key_rows, value_rows, weight, half_weights)
            .astype(jnp.bfloat16)
            .astype(jnp.float32)
        )
        return (apply_net(query_rows, half_weights), partial_value)

    def skip_terms(video_slot, state):
        return (
            jnp.zeros((tok_rows, head_width), jnp.bfloat16),
            jnp.zeros(state_shape, jnp.float32),
        )

    final_shape = (video_count,) + tuple(state_shape)

    def step(turn_index, carry):
        incoming, outputs, finals = carry
        video_index = turn_index - seq_place
        active = (video_index >= 0) & (video_index < video_count)
        video_slot = jnp.clip(video_index, 0, video_count - 1)
        state = jnp.where(seq_place == 0, init_weights, incoming)
        out_rows, partial_value = lax.cond(active, local_terms, skip_terms, video_slot, state)
        padded = pad_slots(partial_value, slot_total)
        owned = lax.psum_scatter(
            padded.astype(jnp.bfloat16), "inner", scatter_dimension=0, tiled=True
        ).astype(jnp.float32)
        mine = lax.cond(active, ortho_all, ortho_none, owned)
        ortho = lax.all_gather(mine, "inner", axis=0, tiled=True)[: state_shape[0]]
        old_out = lax.dynamic_index_in_dim(outputs, video_slot, 0, keepdims=False)
        outputs = lax.dynamic_update_index_in_dim(
            outputs, jnp.where(active, out_rows, old_out), video_slot, 0
        )
        store = active & (seq_place == seq_count - 1)
        old_final = lax.dynamic_index_in_dim(finals, video_slot, 0, keepdims=False)
        new_state = renorm(state, state - step_size * ortho.astype(jnp.float32))
        finals = lax.dynamic_update_index_in_dim(
            finals, jnp.where(store, new_state, old_final), video_slot, 0
        )
        incoming = shifted(new_state, "seq", 1)
        return (incoming, outputs, finals)

    start_carry = (
        jnp.zeros(state_shape, jnp.float32),
        jnp.zeros(queries.shape, jnp.bfloat16),
        jnp.zeros(final_shape, jnp.float32),
    )
    last_in, outputs, finals = lax.fori_loop(0, video_count + seq_count - 1, step, start_carry)
    everything = broadcast(finals, "seq", seq_count - 1)
    row_count = head_width // seq_count
    return (outputs, lax.dynamic_slice_in_dim(everything, seq_place * row_count, row_count, 2))


def solution(mesh):
    in_specs = (
        P(("groups", "batch"), ("seq", "inner"), None),
        P(("groups", "batch"), ("seq", "inner"), None),
        P(("groups", "batch"), ("seq", "inner"), None),
        P(("groups", "batch"), ("seq", "inner")),
        P(("groups", "batch")),
        P(("groups", "batch"), "seq"),
        P(),
    )
    out_specs = (
        P(("groups", "batch"), ("seq", "inner"), None),
        P(("groups", "batch"), None, "seq", None),
    )
    return jax.shard_map(
        per_device, mesh=mesh, in_specs=in_specs, out_specs=out_specs, check_vma=False
    )
```

profile of v0, /device:TPU:0, one launch (start us, length us, event | category | flops | bytes accessed | tf_op | source)
XLA Modules:
  0.0 295.1 jit_solution(18334689422847363460)
XLA Ops:
  8.2 1.0 copy-done
  9.2 222.7 %while.19 = (s32[]{:T(128)}, f32[3,256,256]{2,1,0:T(8,128)S(1)}, bf16[1,256,256]{2,1,0:T(8,128)(2,1)S(1)}, f32[1,3,256,256]{3,2,1,0:T(8,128)S(1)}, pred[]{:T(512...) while((s32[]{:T(128)}, f32[3,256,256]{2,1,0:T(8,128)S(1)}, ...), condition=%wide.region_9.10_spmd.clone, body=%wide.region_0.9_spmd.clone.sunk | while | flops 4337240064 | bytes 41312808 | solution.py:156
  9.3 5.0 %conditional.6 = (bf16[256,256]{1,0:T(8,128)(2,1)S(1)}, bf16[3,256,256]{1,2,0:T(8,128)(2,1)S(1)}) conditional(s32[]{:T(128)} %convert_element_type.135, () %tuple.73, (bf16[1,256,256]{2,1,0:T(8,128)(2,1)}, f32[3,256,256]{2,1,0:T(8,128)S(1)}, s32[]{:T(128)}, s32[256]{0:T(256)S(1)}, s32[1]{0:T(128)}, /*index=5*/s32[1,1]{1,0:T(1,128)}, ...), branch_computations={%region_1.1_spmd, %region_2.2_spmd} | conditional | flops 305202688 | bytes 8524900 | solution.py:131
  9.4 1.3 and_select_fusion
  10.7 0.2 fusion.23
  10.9 0.7 copy-done.5
  11.6 0.2 fusion.19
  11.8 0.3 fusion.4
  12.1 0.2 fusion.25
  12.3 0.3 fusion.3
  12.6 0.3 fusion.5
  13.0 0.8 copy-done.4
  13.8 0.2 fusion.29
  14.0 0.3 convolution_convert_fusion.3
  14.3 0.2 copy.15
  14.5 0.8 concatenate.7
  15.4 14.5 %reduce-scatter.2.cloned.1.call-done = bf16[2,256,256]{2,1,0:T(8,128)(2,1)} async-done(((bf16[4,256,256]{2,1,0:T(8,128)(2,1)}), bf16[2,256,256]{2,1,0:T(8,128)(2,1)}) %reduce-scatter.2.cloned.1.call-update) | async-done | bytes 262160 | tf_op jit(solution)/shard_map/while/body/eval_jaxpr/reduce_scatter | solution.py:133
  29.8 1.0 convert_element_type.136
  30.8 7.2 %conditional.7 = (bf16[2,256,256]{2,1,0:T(8,128)(2,1)S(1)}) conditional(s32[]{:T(128)} %convert_element_type.135, () %tuple.72, f32[2,256,256]{2,1,0:T(8,128)S(1)} %convert_element_type.136), branch_computations={%region_4.4_spmd, %region_5.6_spmd} | conditional | flops 4029284352 | bytes 13369392 | solution.py:136
  31.0 0.8 fusion.46
  31.8 0.8 fusion.44
  32.6 0.7 fusion.51
  33.2 0.7 fusion.43
  33.9 0.7 fusion.52
  34.6 0.7 fusion.42
  35.3 0.7 fusion.53
  35.9 0.7 fusion.41
  36.6 0.7 fusion.54
  37.3 0.7 fusion.45
  38.0 8.6 %all_gather.10 = bf16[4,256,256]{2,1,0:T(8,128)(2,1)S(1)} all-gather(bf16[2,256,256]{2,1,0:T(8,128)(2,1)S(1)} %get-tuple-element.569), channel_id=1, replica_groups=mesh['groups'=2,'seq'=4,'inner'=2,'batch'=2] {'inner'}, dimensions={0}, use_global_device_ids=true | all-gather | bytes 786432 | tf_op jit(solution)/shard_map/while/body/eval_jaxpr/all_gather | solution.py:137
  46.5 0.2 multiply_reduce_fusion.4
  46.8 1.3 fusion.74
  48.0 1.3 collective-permute-start
  49.4 16.3 %collective-permute-done = f32[3,256,256]{2,1,0:T(8,128)S(1)} collective-permute-done((f32[3,256,256]{2,1,0:T(8,128)}, f32[3,256,256]{2,1,0:T(8,128)S(1)}, u32[]{:S(2)}, u32[]{:S(2)}) %collective-permute-start) | collective-permute-done | bytes 786464 | tf_op jit(solution)/shard_map/while/body/eval_jaxpr/ppermute | solution.py:15
  65.9 0.2 copy.15
  66.0 0.8 concatenate.7
  66.9 18.8 %reduce-scatter.2.cloned.1.call-done = bf16[2,256,256]{2,1,0:T(8,128)(2,1)} async-done(((bf16[4,256,256]{2,1,0:T(8,128)(2,1)}), bf16[2,256,256]{2,1,0:T(8,128)(2,1)}) %reduce-scatter.2.cloned.1.call-update) | async-done | bytes 262160 | tf_op jit(solution)/shard_map/while/body/eval_jaxpr/reduce_scatter | solution.py:133
  85.7 1.0 convert_element_type.136
  86.7 8.6 %all_gather.10 = bf16[4,256,256]{2,1,0:T(8,128)(2,1)S(1)} all-gather(bf16[2,256,256]{2,1,0:T(8,128)(2,1)S(1)} %get-tuple-element.569), channel_id=1, replica_groups=mesh['groups'=2,'seq'=4,'inner'=2,'batch'=2] {'inner'}, dimensions={0}, use_global_device_ids=true | all-gather | bytes 786432 | tf_op jit(solution)/shard_map/while/body/eval_jaxpr/all_gather | solution.py:137
  95.3 0.2 multiply_reduce_fusion.4
  95.5 1.3 fusion.74
  96.8 10.5 %collective-permute-start = (f32[3,256,256]{2,1,0:T(8,128)}, f32[3,256,256]{2,1,0:T(8,128)S(1)}, u32[]{:S(2)}, u32[]{:S(2)}) collective-permute-start(f32[3,256,256]{2,1,0:T(8,128)} %get-tuple-element.508), channel_id=1, source_target_pairs={{0,4},{4,8},{8,12},{1,5},{5,9},{9,13},{2,6},{6,10},{10,14},{3,7},{... | collective-permute-start | bytes 2359304 | tf_op jit(solution)/shard_map/while/body/eval_jaxpr/ppermute | solution.py:15
  107.3 16.0 %collective-permute-done = f32[3,256,256]{2,1,0:T(8,128)S(1)} collective-permute-done((f32[3,256,256]{2,1,0:T(8,128)}, f32[3,256,256]{2,1,0:T(8,128)S(1)}, u32[]{:S(2)}, u32[]{:S(2)}) %collective-permute-start) | collective-permute-done | bytes 786464 | tf_op jit(solution)/shard_map/while/body/eval_jaxpr/ppermute | solution.py:15
  123.5 0.2 copy.15
  123.7 0.8 concatenate.7
  124.5 18.5 %reduce-scatter.2.cloned.1.call-done = bf16[2,256,256]{2,1,0:T(8,128)(2,1)} async-done(((bf16[4,256,256]{2,1,0:T(8,128)(2,1)}), bf16[2,256,256]{2,1,0:T(8,128)(2,1)}) %reduce-scatter.2.cloned.1.call-update) | async-done | bytes 262160 | tf_op jit(solution)/shard_map/while/body/eval_jaxpr/reduce_scatter | solution.py:133
  143.1 1.0 convert_element_type.136
  144.1 8.6 %all_gather.10 = bf16[4,256,256]{2,1,0:T(8,128)(2,1)S(1)} all-gather(bf16[2,256,256]{2,1,0:T(8,128)(2,1)S(1)} %get-tuple-element.569), channel_id=1, replica_groups=mesh['groups'=2,'seq'=4,'inner'=2,'batch'=2] {'inner'}, dimensions={0}, use_global_device_ids=true | all-gather | bytes 786432 | tf_op jit(solution)/shard_map/while/body/eval_jaxpr/all_gather | solution.py:137
  152.7 0.2 multiply_reduce_fusion.4
  152.9 1.3 fusion.74
  154.1 3.4 %collective-permute-start = (f32[3,256,256]{2,1,0:T(8,128)}, f32[3,256,256]{2,1,0:T(8,128)S(1)}, u32[]{:S(2)}, u32[]{:S(2)}) collective-permute-start(f32[3,256,256]{2,1,0:T(8,128)} %get-tuple-element.508), channel_id=1, source_target_pairs={{0,4},{4,8},{8,12},{1,5},{5,9},{9,13},{2,6},{6,10},{10,14},{3,7},{... | collective-permute-start | bytes 2359304 | tf_op jit(solution)/shard_map/while/body/eval_jaxpr/ppermute | solution.py:15
  157.6 16.0 %collective-permute-done = f32[3,256,256]{2,1,0:T(8,128)S(1)} collective-permute-done((f32[3,256,256]{2,1,0:T(8,128)}, f32[3,256,256]{2,1,0:T(8,128)S(1)}, u32[]{:S(2)}, u32[]{:S(2)}) %collective-permute-start) | collective-permute-done | bytes 786464 | tf_op jit(solution)/shard_map/while/body/eval_jaxpr/ppermute | solution.py:15
  173.8 0.2 copy.15
  174.0 0.8 concatenate.7
  174.8 26.5 %reduce-scatter.2.cloned.1.call-done = bf16[2,256,256]{2,1,0:T(8,128)(2,1)} async-done(((bf16[4,256,256]{2,1,0:T(8,128)(2,1)}), bf16[2,256,256]{2,1,0:T(8,128)(2,1)}) %reduce-scatter.2.cloned.1.call-update) | async-done | bytes 262160 | tf_op jit(solution)/shard_map/while/body/eval_jaxpr/reduce_scatter | solution.py:133
  201.4 1.0 convert_element_type.136
  202.4 8.5 %all_gather.10 = bf16[4,256,256]{2,1,0:T(8,128)(2,1)S(1)} all-gather(bf16[2,256,256]{2,1,0:T(8,128)(2,1)S(1)} %get-tuple-element.569), channel_id=1, replica_groups=mesh['groups'=2,'seq'=4,'inner'=2,'batch'=2] {'inner'}, dimensions={0}, use_global_device_ids=true | all-gather | bytes 786432 | tf_op jit(solution)/shard_map/while/body/eval_jaxpr/all_gather | solution.py:137
  210.9 0.2 multiply_reduce_fusion.4
  211.2 1.3 fusion.74
  212.4 3.4 %collective-permute-start = (f32[3,256,256]{2,1,0:T(8,128)}, f32[3,256,256]{2,1,0:T(8,128)S(1)}, u32[]{:S(2)}, u32[]{:S(2)}) collective-permute-start(f32[3,256,256]{2,1,0:T(8,128)} %get-tuple-element.508), channel_id=1, source_target_pairs={{0,4},{4,8},{8,12},{1,5},{5,9},{9,13},{2,6},{6,10},{10,14},{3,7},{... | collective-permute-start | bytes 2359304 | tf_op jit(solution)/shard_map/while/body/eval_jaxpr/ppermute | solution.py:15
  215.9 16.0 %collective-permute-done = f32[3,256,256]{2,1,0:T(8,128)S(1)} collective-permute-done((f32[3,256,256]{2,1,0:T(8,128)}, f32[3,256,256]{2,1,0:T(8,128)S(1)}, u32[]{:S(2)}, u32[]{:S(2)}) %collective-permute-start) | collective-permute-done | bytes 786464 | tf_op jit(solution)/shard_map/while/body/eval_jaxpr/ppermute | solution.py:15
  231.9 1.0 broadcast_select_fusion.1
  232.9 53.5 %all-reduce.3.cloned.1.call-done = f32[1,3,256,256]{3,2,1,0:T(8,128)} async-done(((f32[1,3,256,256]{3,2,1,0:T(8,128)}), f32[1,3,256,256]{3,2,1,0:T(8,128)}) %all-reduce.3.cloned.1.call-update) | async-done | bytes 786448 | tf_op jit(solution)/shard_map/psum | solution.py:20
  286.4 1.6 constant_dynamic-slice_fusion
  (65 shorter events, 1.7 us)
Async XLA Ops:
  8.0 1.1 copy-start
  8.1 1.1 copy-start.2
  8.1 1.1 copy-start.6
  9.2 20.6 %reduce-scatter.2.cloned.1.call-start = ((), (), s32[]{:S(2)}) async-start(), calls=%async_computation.2 | async-start | bytes 786432 | tf_op jit(solution)/shard_map/while/body/eval_jaxpr/reduce_scatter | solution.py:133
  10.7 0.9 copy-start.5
  12.9 0.9 copy-start.4
  46.8 18.9 %copy-start.1 = (f32[3,256,256]{2,1,0:T(8,128)S(1)}, f32[3,256,256]{2,1,0:T(8,128)}, u32[]{:S(2)}) copy-start(f32[3,256,256]{2,1,0:T(8,128)} %get-tuple-element.593) | copy-start | bytes 2359300 | tf_op jit(solution)/shard_map/while
  48.0 17.6 %collective-permute-start = (f32[3,256,256]{2,1,0:T(8,128)}, f32[3,256,256]{2,1,0:T(8,128)S(1)}, u32[]{:S(2)}, u32[]{:S(2)}) collective-permute-start(f32[3,256,256]{2,1,0:T(8,128)} %get-tuple-element.508), channel_id=1, source_target_pairs={{0,4},{4,8},{8,12},{1,5},{5,9},{9,13},{2,6},{6,10},{10,14},{3,7},{... | collective-permute-start | bytes 2359304 | tf_op jit(solution)/shard_map/while/body/eval_jaxpr/ppermute | solution.py:15
  65.7 20.0 %reduce-scatter.2.cloned.1.call-start = ((), (), s32[]{:S(2)}) async-start(), calls=%async_computation.2 | async-start | bytes 786432 | tf_op jit(solution)/shard_map/while/body/eval_jaxpr/reduce_scatter | solution.py:133
  95.5 27.8 %copy-start.1 = (f32[3,256,256]{2,1,0:T(8,128)S(1)}, f32[3,256,256]{2,1,0:T(8,128)}, u32[]{:S(2)}) copy-start(f32[3,256,256]{2,1,0:T(8,128)} %get-tuple-element.593) | copy-start | bytes 2359300 | tf_op jit(solution)/shard_map/while
  96.8 26.5 %collective-permute-start = (f32[3,256,256]{2,1,0:T(8,128)}, f32[3,256,256]{2,1,0:T(8,128)S(1)}, u32[]{:S(2)}, u32[]{:S(2)}) collective-permute-start(f32[3,256,256]{2,1,0:T(8,128)} %get-tuple-element.508), channel_id=1, source_target_pairs={{0,4},{4,8},{8,12},{1,5},{5,9},{9,13},{2,6},{6,10},{10,14},{3,7},{... | collective-permute-start | bytes 2359304 | tf_op jit(solution)/shard_map/while/body/eval_jaxpr/ppermute | solution.py:15
  123.3 19.8 %reduce-scatter.2.cloned.1.call-start = ((), (), s32[]{:S(2)}) async-start(), calls=%async_computation.2 | async-start | bytes 786432 | tf_op jit(solution)/shard_map/while/body/eval_jaxpr/reduce_scatter | solution.py:133
  152.9 20.7 %copy-start.1 = (f32[3,256,256]{2,1,0:T(8,128)S(1)}, f32[3,256,256]{2,1,0:T(8,128)}, u32[]{:S(2)}) copy-start(f32[3,256,256]{2,1,0:T(8,128)} %get-tuple-element.593) | copy-start | bytes 2359300 | tf_op jit(solution)/shard_map/while
  154.1 19.5 %collective-permute-start = (f32[3,256,256]{2,1,0:T(8,128)}, f32[3,256,256]{2,1,0:T(8,128)S(1)}, u32[]{:S(2)}, u32[]{:S(2)}) collective-permute-start(f32[3,256,256]{2,1,0:T(8,128)} %get-tuple-element.508), channel_id=1, source_target_pairs={{0,4},{4,8},{8,12},{1,5},{5,9},{9,13},{2,6},{6,10},{10,14},{3,7},{... | collective-permute-start | bytes 2359304 | tf_op jit(solution)/shard_map/while/body/eval_jaxpr/ppermute | solution.py:15
  173.6 27.8 %reduce-scatter.2.cloned.1.call-start = ((), (), s32[]{:S(2)}) async-start(), calls=%async_computation.2 | async-start | bytes 786432 | tf_op jit(solution)/shard_map/while/body/eval_jaxpr/reduce_scatter | solution.py:133
  211.1 20.8 %copy-start.1 = (f32[3,256,256]{2,1,0:T(8,128)S(1)}, f32[3,256,256]{2,1,0:T(8,128)}, u32[]{:S(2)}) copy-start(f32[3,256,256]{2,1,0:T(8,128)} %get-tuple-element.593) | copy-start | bytes 2359300 | tf_op jit(solution)/shard_map/while
  212.4 19.5 %collective-permute-start = (f32[3,256,256]{2,1,0:T(8,128)}, f32[3,256,256]{2,1,0:T(8,128)S(1)}, u32[]{:S(2)}, u32[]{:S(2)}) collective-permute-start(f32[3,256,256]{2,1,0:T(8,128)} %get-tuple-element.508), channel_id=1, source_target_pairs={{0,4},{4,8},{8,12},{1,5},{5,9},{9,13},{2,6},{6,10},{10,14},{3,7},{... | collective-permute-start | bytes 2359304 | tf_op jit(solution)/shard_map/while/body/eval_jaxpr/ppermute | solution.py:15
  231.9 1.0 copy-start.3
  231.9 54.5 %all-reduce.3.cloned.1.call-start = ((), (), s32[]{:S(2)}) async-start(), calls=%async_computation.1 | async-start | bytes 1572864 | tf_op jit(solution)/shard_map/psum | solution.py:20
Sparse Core Ops, SparseCore 0:
  15.5 14.2 reduce-scatter.1
  68.7 16.9 reduce-scatter.1
  126.3 16.6 reduce-scatter.1
  176.3 24.9 reduce-scatter.1
Sparse Core Ops, SparseCore 1:
  234.7 51.6 all-reduce.2
where the time goes:
time: 296 us; the launch traced here: 295 us
  waiting for transfers between devices  196 us (66%)
  blocking collectives  34.2 us (12%)
  starting transfers between devices  18.7 us (6%)
  between operations  15.2 us (5%)
  other arithmetic  12.9 us (4%)
  matrix products  8.87 us (3%)
  local copies, waits for them, and re-layouts  8.5 us (3%)
    reduce_scatter x4, waiting for transfers between devices, step(): lax.psum_scatter(padded.astype(jnp.bfloat16), 'inner', scatter_dimension=...  78.3 us
    ppermute x4, waiting for transfers between devices, shifted(): lax.ppermute(value, axis, [(source, source + steps) for source in range(i...  64.2 us
    psum x1, waiting for transfers between devices, broadcast(): return lax.psum(jnp.where(mine, value, jnp.zeros_like(value)), axis)  53.5 us
    all_gather x4, blocking collectives, step(): ortho = lax.all_gather(mine, 'inner', axis=0, tiled=True)[:state_shape[0]]  34.2 us
    ppermute x4, starting transfers between devices, shifted(): lax.ppermute(value, axis, [(source, source + steps) for source in range(i...  18.7 us
  transfers between devices with their start and end apart: 9, of which 9 were waited for; matrix products, arithmetic and copies ran while one was open for 0% of the time, Pallas kernels for 0%

commit v1 on v0

--- a/solution.py
+++ b/solution.py
@@ -2,11 +2,24 @@
 import jax.numpy as jnp
 from jax import lax
 from jax.sharding import PartitionSpec as P
+from jax.lax import axis_index, ppermute, psum
 
 NS_STEPS = 5
 step_size = 0.1
 norm_eps = 1e-07
 column_eps = 1e-06
+
+
+def build_vector(t0, comm_axis):
+    reply, plain = (psum(1, comm_axis), axis_index(comm_axis))
+    y1, item_now = (t0, 1)
+    while item_now < reply:
+        big = ppermute(y1, axis_name=comm_axis, perm=[(j, j ^ item_now) for j in range(reply)])
+        new = jnp.concatenate([y1, big], axis=0)
+        state_next = jnp.concatenate([big, y1], axis=0)
+        y1 = jnp.where(plain & item_now == 0, new, state_next)
+        item_now = 2 * item_now
+    return y1
 
 
 def shifted(value, axis, steps):
@@ -134,7 +147,7 @@
             padded.astype(jnp.bfloat16), "inner", scatter_dimension=0, tiled=True
         ).astype(jnp.float32)
         mine = lax.cond(active, ortho_all, ortho_none, owned)
-        ortho = lax.all_gather(mine, "inner", axis=0, tiled=True)[: state_shape[0]]
+        ortho = build_vector(mine, "inner")[: state_shape[0]]
         old_out = lax.dynamic_index_in_dim(outputs, video_slot, 0, keepdims=False)
         outputs = lax.dynamic_update_index_in_dim(
             outputs, jnp.where(active, out_rows, old_out), video_slot, 0

time: 296 us -> 289 us (0.976)
  blocking collectives: 34.2 us -> 0 us
  waiting for transfers between devices: 196 us -> 218 us
  other arithmetic: 12.9 us -> 17.7 us
    all_gather x4 -> x0, blocking collectives: 34.2 us -> none  [step(): ortho = lax.all_gather(mine, 'inner', axis=0, tiled=True)[:state_shape[0]]]
    ppermute x0 -> x4, waiting for transfers between devices: none -> 30.1 us  [build_vector(): ppermute(y1, axis_name=comm_axis, perm=[(j, j ^ item_now) for j in range(...]
    reduce_scatter x4, waiting for transfers between devices: 78.3 us -> 70.4 us  [step(): lax.psum_scatter(padded.astype(jnp.bfloat16), 'inner', scatter_dimension=...]
    select_n x4, other arithmetic: 0.4 us -> 4.94 us  [step(): state = jnp.where(seq_place == 0, init_weights, incoming)]
  transfers between devices with their start and end apart: 9 -> 13, of which waited for: 9 -> 13; matrix products, arithmetic and copies ran while one was open for 0% -> 0% of each run, Pallas kernels for 0% -> 0%
where the time goes in v1:
time: 289 us; the launch traced here: 288 us
  waiting for transfers between devices  218 us (75%)
  starting transfers between devices  20.4 us (7%)
  other arithmetic  17.7 us (6%)
  between operations  15.2 us (5%)
  matrix products  8.87 us (3%)
  local copies, waits for them, and re-layouts  6.91 us (2%)
    reduce_scatter x4, waiting for transfers between devices, step(): lax.psum_scatter(padded.astype(jnp.bfloat16), 'inner', scatter_dimension=...  70.4 us
    ppermute x4, waiting for transfers between devices, shifted(): lax.ppermute(value, axis, [(source, source + steps) for source in range(i...  64.2 us
    psum x1, waiting for transfers between devices, broadcast(): return lax.psum(jnp.where(mine, value, jnp.zeros_like(value)), axis)  53.5 us
    ppermute x4, waiting for transfers between devices, build_vector(): ppermute(y1, axis_name=comm_axis, perm=[(j, j ^ item_now) for j in range(...  30.1 us
    ppermute x4, starting transfers between devices, shifted(): lax.ppermute(value, axis, [(source, source + steps) for source in range(i...  18.8 us
  transfers between devices with their start and end apart: 13, of which 13 were waited for; matrix products, arithmetic and copies ran while one was open for 0% of the time, Pallas kernels for 0%

profile of v1, /device:TPU:0, one launch (start us, length us, event | category | flops | bytes accessed | tf_op | source)
XLA Modules:
  0.0 288.0 jit_solution(16502594014466152601)
XLA Ops:
  8.2 0.8 copy-done
  9.1 215.7 %while.19 = (s32[]{:T(128)}, f32[3,256,256]{2,1,0:T(8,128)S(1)}, bf16[1,256,256]{2,1,0:T(8,128)(2,1)S(1)}, f32[1,3,256,256]{3,2,1,0:T(8,128)S(1)}, pred[]{:T(512...) while((s32[]{:T(128)}, f32[3,256,256]{2,1,0:T(8,128)S(1)}, ...), condition=%wide.region_9.10_spmd.clone, body=%wide.region_0.9_spmd.clone.sunk | while | flops 4338419712 | bytes 37642800 | solution.py:169
  9.1 1.2 broadcast_select_fusion.3
  10.4 3.5 %conditional.6 = (bf16[256,256]{1,0:T(8,128)(2,1)S(1)}, bf16[3,256,256]{1,2,0:T(8,128)(2,1)S(1)}) conditional(s32[]{:T(128)} %convert_element_type.135, () %tuple.73, (bf16[1,256,256]{2,1,0:T(8,128)(2,1)S(1)}, f32[3,256,256]{2,1,0:T(8,128)S(1)}, s32[]{:T(128)}, s32[256]{0:T(256)S(1)}, s32[1]{0:T(128)}, /*index=5*/s32[1,1]{1,0:T(1,128)}, ...), branch_computations={%region_1.1_spmd, %region_2.2_spmd} | conditional | flops 305202688 | bytes 7476268 | solution.py:144
  10.5 1.3 and_select_fusion
  11.9 0.2 fusion.19
  12.2 0.3 fusion.4
  12.5 0.2 fusion.25
  12.7 0.3 fusion.3
  13.0 0.3 fusion.5
  13.5 0.3 convolution_convert_fusion.3
  14.0 0.8 concatenate.25
  14.9 14.7 %reduce-scatter.2.cloned.1.call-done = bf16[2,256,256]{2,1,0:T(8,128)(2,1)} async-done(((bf16[4,256,256]{2,1,0:T(8,128)(2,1)}), bf16[2,256,256]{2,1,0:T(8,128)(2,1)}) %reduce-scatter.2.cloned.1.call-update) | async-done | bytes 262160 | tf_op jit(solution)/shard_map/while/body/eval_jaxpr/reduce_scatter | solution.py:146
  29.5 1.0 convert_element_type.136
  30.5 7.2 %conditional.7 = (bf16[2,256,256]{2,1,0:T(8,128)(2,1)S(1)}) conditional(s32[]{:T(128)} %convert_element_type.135, () %tuple.72, f32[2,256,256]{2,1,0:T(8,128)S(1)} %convert_element_type.136), branch_computations={%region_4.4_spmd, %region_5.6_spmd} | conditional | flops 4029284352 | bytes 13369392 | solution.py:149
  30.7 0.8 fusion.46
  31.5 0.8 fusion.44
  32.3 0.7 fusion.52
  32.9 0.7 fusion.43
  33.6 0.7 fusion.53
  34.3 0.7 fusion.42
  35.0 0.7 fusion.54
  35.7 0.7 fusion.41
  36.4 0.7 fusion.55
  37.0 0.7 fusion.45
  37.7 0.4 collective-permute-start
  38.1 7.5 %collective-permute-done = bf16[2,256,256]{2,1,0:T(8,128)(2,1)S(1)} collective-permute-done((bf16[2,256,256]{2,1,0:T(8,128)(2,1)S(1)}, bf16[2,256,256]{2,1,0:T(8,128)(2,1)S(1)}, u32[]{:S(2)}, u32[]{:S(2)}) %collective-permute-start) | collective-permute-done | bytes 262176 | tf_op jit(solution)/shard_map/while/body/eval_jaxpr/ppermute | solution.py:17
  45.7 0.2 multiply_reduce_fusion.4
  45.9 1.3 fusion.75
  47.2 1.3 collective-permute-start.1
  48.6 16.3 %collective-permute-done.1 = f32[3,256,256]{2,1,0:T(8,128)S(1)} collective-permute-done((f32[3,256,256]{2,1,0:T(8,128)}, f32[3,256,256]{2,1,0:T(8,128)S(1)}, u32[]{:S(2)}, u32[]{:S(2)}) %collective-permute-start.1) | collective-permute-done | bytes 786464 | tf_op jit(solution)/shard_map/while/body/eval_jaxpr/ppermute | solution.py:28
  64.9 1.2 broadcast_select_fusion.3
  66.4 0.8 concatenate.25
  67.2 16.1 %reduce-scatter.2.cloned.1.call-done = bf16[2,256,256]{2,1,0:T(8,128)(2,1)} async-done(((bf16[4,256,256]{2,1,0:T(8,128)(2,1)}), bf16[2,256,256]{2,1,0:T(8,128)(2,1)}) %reduce-scatter.2.cloned.1.call-update) | async-done | bytes 262160 | tf_op jit(solution)/shard_map/while/body/eval_jaxpr/reduce_scatter | solution.py:146
  83.3 1.0 convert_element_type.136
  84.3 0.4 collective-permute-start
  84.8 7.5 %collective-permute-done = bf16[2,256,256]{2,1,0:T(8,128)(2,1)S(1)} collective-permute-done((bf16[2,256,256]{2,1,0:T(8,128)(2,1)S(1)}, bf16[2,256,256]{2,1,0:T(8,128)(2,1)S(1)}, u32[]{:S(2)}, u32[]{:S(2)}) %collective-permute-start) | collective-permute-done | bytes 262176 | tf_op jit(solution)/shard_map/while/body/eval_jaxpr/ppermute | solution.py:17
  92.3 0.2 multiply_reduce_fusion.4
  92.5 1.3 fusion.75
  93.8 10.6 %collective-permute-start.1 = (f32[3,256,256]{2,1,0:T(8,128)}, f32[3,256,256]{2,1,0:T(8,128)S(1)}, u32[]{:S(2)}, u32[]{:S(2)}) collective-permute-start(f32[3,256,256]{2,1,0:T(8,128)} %get-tuple-element.508), channel_id=1, source_target_pairs={{0,4},{4,8},{8,12},{1,5},{5,9},{9,13},{2,6},{6,10},{10,14},{3,7},{... | collective-permute-start | bytes 2359304 | tf_op jit(solution)/shard_map/while/body/eval_jaxpr/ppermute | solution.py:28
  104.4 16.0 %collective-permute-done.1 = f32[3,256,256]{2,1,0:T(8,128)S(1)} collective-permute-done((f32[3,256,256]{2,1,0:T(8,128)}, f32[3,256,256]{2,1,0:T(8,128)S(1)}, u32[]{:S(2)}, u32[]{:S(2)}) %collective-permute-start.1) | collective-permute-done | bytes 786464 | tf_op jit(solution)/shard_map/while/body/eval_jaxpr/ppermute | solution.py:28
  120.4 1.2 broadcast_select_fusion.3
  121.9 0.8 concatenate.25
  122.8 15.8 %reduce-scatter.2.cloned.1.call-done = bf16[2,256,256]{2,1,0:T(8,128)(2,1)} async-done(((bf16[4,256,256]{2,1,0:T(8,128)(2,1)}), bf16[2,256,256]{2,1,0:T(8,128)(2,1)}) %reduce-scatter.2.cloned.1.call-update) | async-done | bytes 262160 | tf_op jit(solution)/shard_map/while/body/eval_jaxpr/reduce_scatter | solution.py:146
  138.6 1.0 convert_element_type.136
  139.6 0.4 collective-permute-start
  140.0 7.5 %collective-permute-done = bf16[2,256,256]{2,1,0:T(8,128)(2,1)S(1)} collective-permute-done((bf16[2,256,256]{2,1,0:T(8,128)(2,1)S(1)}, bf16[2,256,256]{2,1,0:T(8,128)(2,1)S(1)}, u32[]{:S(2)}, u32[]{:S(2)}) %collective-permute-start) | collective-permute-done | bytes 262176 | tf_op jit(solution)/shard_map/while/body/eval_jaxpr/ppermute | solution.py:17
  147.6 0.2 multiply_reduce_fusion.4
  147.8 1.3 fusion.75
  149.1 3.4 %collective-permute-start.1 = (f32[3,256,256]{2,1,0:T(8,128)}, f32[3,256,256]{2,1,0:T(8,128)S(1)}, u32[]{:S(2)}, u32[]{:S(2)}) collective-permute-start(f32[3,256,256]{2,1,0:T(8,128)} %get-tuple-element.508), channel_id=1, source_target_pairs={{0,4},{4,8},{8,12},{1,5},{5,9},{9,13},{2,6},{6,10},{10,14},{3,7},{... | collective-permute-start | bytes 2359304 | tf_op jit(solution)/shard_map/while/body/eval_jaxpr/ppermute | solution.py:28
  152.6 16.0 %collective-permute-done.1 = f32[3,256,256]{2,1,0:T(8,128)S(1)} collective-permute-done((f32[3,256,256]{2,1,0:T(8,128)}, f32[3,256,256]{2,1,0:T(8,128)S(1)}, u32[]{:S(2)}, u32[]{:S(2)}) %collective-permute-start.1) | collective-permute-done | bytes 786464 | tf_op jit(solution)/shard_map/while/body/eval_jaxpr/ppermute | solution.py:28
  168.6 1.2 broadcast_select_fusion.3
  170.1 0.8 concatenate.25
  170.9 23.9 %reduce-scatter.2.cloned.1.call-done = bf16[2,256,256]{2,1,0:T(8,128)(2,1)} async-done(((bf16[4,256,256]{2,1,0:T(8,128)(2,1)}), bf16[2,256,256]{2,1,0:T(8,128)(2,1)}) %reduce-scatter.2.cloned.1.call-update) | async-done | bytes 262160 | tf_op jit(solution)/shard_map/while/body/eval_jaxpr/reduce_scatter | solution.py:146
  194.8 1.0 convert_element_type.136
  195.9 0.4 collective-permute-start
  196.2 7.5 %collective-permute-done = bf16[2,256,256]{2,1,0:T(8,128)(2,1)S(1)} collective-permute-done((bf16[2,256,256]{2,1,0:T(8,128)(2,1)S(1)}, bf16[2,256,256]{2,1,0:T(8,128)(2,1)S(1)}, u32[]{:S(2)}, u32[]{:S(2)}) %collective-permute-start) | collective-permute-done | bytes 262176 | tf_op jit(solution)/shard_map/while/body/eval_jaxpr/ppermute | solution.py:17
  203.8 0.2 multiply_reduce_fusion.4
  204.0 1.3 fusion.75
  205.3 3.4 %collective-permute-start.1 = (f32[3,256,256]{2,1,0:T(8,128)}, f32[3,256,256]{2,1,0:T(8,128)S(1)}, u32[]{:S(2)}, u32[]{:S(2)}) collective-permute-start(f32[3,256,256]{2,1,0:T(8,128)} %get-tuple-element.508), channel_id=1, source_target_pairs={{0,4},{4,8},{8,12},{1,5},{5,9},{9,13},{2,6},{6,10},{10,14},{3,7},{... | collective-permute-start | bytes 2359304 | tf_op jit(solution)/shard_map/while/body/eval_jaxpr/ppermute | solution.py:28
  208.8 16.0 %collective-permute-done.1 = f32[3,256,256]{2,1,0:T(8,128)S(1)} collective-permute-done((f32[3,256,256]{2,1,0:T(8,128)}, f32[3,256,256]{2,1,0:T(8,128)S(1)}, u32[]{:S(2)}, u32[]{:S(2)}) %collective-permute-start.1) | collective-permute-done | bytes 786464 | tf_op jit(solution)/shard_map/while/body/eval_jaxpr/ppermute | solution.py:28
  224.8 1.0 broadcast_select_fusion.1
  225.8 53.5 %all-reduce.3.cloned.1.call-done = f32[1,3,256,256]{3,2,1,0:T(8,128)} async-done(((f32[1,3,256,256]{3,2,1,0:T(8,128)}), f32[1,3,256,256]{3,2,1,0:T(8,128)}) %all-reduce.3.cloned.1.call-update) | async-done | bytes 786448 | tf_op jit(solution)/shard_map/psum | solution.py:33
  279.3 1.6 constant_dynamic-slice_fusion
  (59 shorter events, 2.4 us)
Async XLA Ops:
  8.1 0.9 copy-start
  8.1 1.0 copy-start.2
  8.1 1.0 copy-start.3
  8.1 1.0 copy-start.4
  9.1 20.4 %reduce-scatter.2.cloned.1.call-start = ((), (), s32[]{:S(2)}) async-start(), calls=%async_computation.2 | async-start | bytes 786432 | tf_op jit(solution)/shard_map/while/body/eval_jaxpr/reduce_scatter | solution.py:146
  37.7 8.0 %collective-permute-start = (bf16[2,256,256]{2,1,0:T(8,128)(2,1)S(1)}, bf16[2,256,256]{2,1,0:T(8,128)(2,1)S(1)}, u32[]{:S(2)}, u32[]{:S(2)}) collective-permute-start(bf16[2,256,256]{2,1,0:T(8,128)(2,1)S(1)} %get-tuple-element.572), channel_id=1, source_target_pairs={{0,2},{2,0},{1,3},{3,1},{4,6},{6,4},{5,7},{7,5},{8,10},{10,8},{9,1... | collective-permute-start | bytes 786440 | tf_op jit(solution)/shard_map/while/body/eval_jaxpr/ppermute | solution.py:17
  47.2 17.7 %collective-permute-start.1 = (f32[3,256,256]{2,1,0:T(8,128)}, f32[3,256,256]{2,1,0:T(8,128)S(1)}, u32[]{:S(2)}, u32[]{:S(2)}) collective-permute-start(f32[3,256,256]{2,1,0:T(8,128)} %get-tuple-element.508), channel_id=1, source_target_pairs={{0,4},{4,8},{8,12},{1,5},{5,9},{9,13},{2,6},{6,10},{10,14},{3,7},{... | collective-permute-start | bytes 2359304 | tf_op jit(solution)/shard_map/while/body/eval_jaxpr/ppermute | solution.py:28
  64.8 18.4 %reduce-scatter.2.cloned.1.call-start = ((), (), s32[]{:S(2)}) async-start(), calls=%async_computation.2 | async-start | bytes 786432 | tf_op jit(solution)/shard_map/while/body/eval_jaxpr/reduce_scatter | solution.py:146
  84.3 7.9 %collective-permute-start = (bf16[2,256,256]{2,1,0:T(8,128)(2,1)S(1)}, bf16[2,256,256]{2,1,0:T(8,128)(2,1)S(1)}, u32[]{:S(2)}, u32[]{:S(2)}) collective-permute-start(bf16[2,256,256]{2,1,0:T(8,128)(2,1)S(1)} %get-tuple-element.572), channel_id=1, source_target_pairs={{0,2},{2,0},{1,3},{3,1},{4,6},{6,4},{5,7},{7,5},{8,10},{10,8},{9,1... | collective-permute-start | bytes 786440 | tf_op jit(solution)/shard_map/while/body/eval_jaxpr/ppermute | solution.py:17
  93.8 26.6 %collective-permute-start.1 = (f32[3,256,256]{2,1,0:T(8,128)}, f32[3,256,256]{2,1,0:T(8,128)S(1)}, u32[]{:S(2)}, u32[]{:S(2)}) collective-permute-start(f32[3,256,256]{2,1,0:T(8,128)} %get-tuple-element.508), channel_id=1, source_target_pairs={{0,4},{4,8},{8,12},{1,5},{5,9},{9,13},{2,6},{6,10},{10,14},{3,7},{... | collective-permute-start | bytes 2359304 | tf_op jit(solution)/shard_map/while/body/eval_jaxpr/ppermute | solution.py:28
  120.4 18.2 %reduce-scatter.2.cloned.1.call-start = ((), (), s32[]{:S(2)}) async-start(), calls=%async_computation.2 | async-start | bytes 786432 | tf_op jit(solution)/shard_map/while/body/eval_jaxpr/reduce_scatter | solution.py:146
  139.6 8.0 %collective-permute-start = (bf16[2,256,256]{2,1,0:T(8,128)(2,1)S(1)}, bf16[2,256,256]{2,1,0:T(8,128)(2,1)S(1)}, u32[]{:S(2)}, u32[]{:S(2)}) collective-permute-start(bf16[2,256,256]{2,1,0:T(8,128)(2,1)S(1)} %get-tuple-element.572), channel_id=1, source_target_pairs={{0,2},{2,0},{1,3},{3,1},{4,6},{6,4},{5,7},{7,5},{8,10},{10,8},{9,1... | collective-permute-start | bytes 786440 | tf_op jit(solution)/shard_map/while/body/eval_jaxpr/ppermute | solution.py:17
  149.1 19.5 %collective-permute-start.1 = (f32[3,256,256]{2,1,0:T(8,128)}, f32[3,256,256]{2,1,0:T(8,128)S(1)}, u32[]{:S(2)}, u32[]{:S(2)}) collective-permute-start(f32[3,256,256]{2,1,0:T(8,128)} %get-tuple-element.508), channel_id=1, source_target_pairs={{0,4},{4,8},{8,12},{1,5},{5,9},{9,13},{2,6},{6,10},{10,14},{3,7},{... | collective-permute-start | bytes 2359304 | tf_op jit(solution)/shard_map/while/body/eval_jaxpr/ppermute | solution.py:28
  168.6 26.3 %reduce-scatter.2.cloned.1.call-start = ((), (), s32[]{:S(2)}) async-start(), calls=%async_computation.2 | async-start | bytes 786432 | tf_op jit(solution)/shard_map/while/body/eval_jaxpr/reduce_scatter | solution.py:146
  195.9 7.9 %collective-permute-start = (bf16[2,256,256]{2,1,0:T(8,128)(2,1)S(1)}, bf16[2,256,256]{2,1,0:T(8,128)(2,1)S(1)}, u32[]{:S(2)}, u32[]{:S(2)}) collective-permute-start(bf16[2,256,256]{2,1,0:T(8,128)(2,1)S(1)} %get-tuple-element.572), channel_id=1, source_target_pairs={{0,2},{2,0},{1,3},{3,1},{4,6},{6,4},{5,7},{7,5},{8,10},{10,8},{9,1... | collective-permute-start | bytes 786440 | tf_op jit(solution)/shard_map/while/body/eval_jaxpr/ppermute | solution.py:17
  205.3 19.5 %collective-permute-start.1 = (f32[3,256,256]{2,1,0:T(8,128)}, f32[3,256,256]{2,1,0:T(8,128)S(1)}, u32[]{:S(2)}, u32[]{:S(2)}) collective-permute-start(f32[3,256,256]{2,1,0:T(8,128)} %get-tuple-element.508), channel_id=1, source_target_pairs={{0,4},{4,8},{8,12},{1,5},{5,9},{9,13},{2,6},{6,10},{10,14},{3,7},{... | collective-permute-start | bytes 2359304 | tf_op jit(solution)/shard_map/while/body/eval_jaxpr/ppermute | solution.py:28
  224.8 1.0 copy-start.1
  224.8 54.5 %all-reduce.3.cloned.1.call-start = ((), (), s32[]{:S(2)}) async-start(), calls=%async_computation.1 | async-start | bytes 1572864 | tf_op jit(solution)/shard_map/psum | solution.py:33
Sparse Core Ops, SparseCore 0:
  15.0 14.4 reduce-scatter.1
  67.9 15.3 reduce-scatter.1
  123.4 15.0 reduce-scatter.1
  171.3 23.4 reduce-scatter.1
Sparse Core Ops, SparseCore 1:
  227.6 51.6 all-reduce.2
